TPU v7x, 32 devices: a whole 2x2x4 slice. The times are simulated.
32 devices in a mesh: groups: 2 (over y), seq: 4 (over z), tp: 2 (over x), kv: 2 (over core).
Axes of the slice: x: 2, y: 2, z: 4, core: 2. Of those that a mesh axis runs over, the one named last changes fastest.
Arguments:
- events: bfloat16 [8, 512, 2048], P('groups', 'seq', ('tp', 'kv')), parts along dimension 0, may hold values from -6 to 6
- history_cache: bfloat16 [2, 8, 512, 1024], P(None, ('groups', 'seq'), None, ('tp', 'kv')), parts along dimension 1, may hold values from -6 to 6
- block_counts: int32 [8], P(('groups', 'seq')), parts along dimension 0, may hold values from 1 to 4
- semantic_ids: int32 [4, 128], P(None, ('groups', 'seq')), parts along dimension 1, may hold values from 0 to 4095
- beam_parents: int32 [3, 128], P(None, ('groups', 'seq')), parts along dimension 1, may hold values from 0 to 15
- query_weight: bfloat16 [2048, 2048], P('seq', ('tp', 'kv')), may hold values from -0.125 to 0.125
- keyval_weight: bfloat16 [2, 2048, 1024], P(None, 'seq', ('tp', 'kv')), may hold values from -0.125 to 0.125
- out_weight: bfloat16 [2048, 2048], P('seq', ('tp', 'kv')), may hold values from -0.125 to 0.125
- cross_weight: bfloat16 [2, 2048, 1024], P(None, 'seq', ('tp', 'kv')), may hold values from -0.125 to 0.125
- decoder_query: bfloat16 [2048, 2048], P(None, ('tp', 'kv')), may hold values from -0.125 to 0.125
- decoder_out: bfloat16 [2048, 2048], P(None, ('tp', 'kv')), may hold values from -0.125 to 0.125
- code_table: bfloat16 [4096, 2048], P(('tp', 'kv')), may hold values from -6 to 6
- encoder_gain: float32 [2048], replicated, may hold values from 0.25 to 1.75
- cross_gain: float32 [2048], replicated, may hold values from 0.25 to 1.75
- decoder_gain: float32 [2048], replicated, may hold values from 0.25 to 1.75
Outputs:
- encoded: bfloat16 [8, 512, 2048], P(('groups', 'seq'), ('tp', 'kv')), parts along dimension 0
- beam_state: bfloat16 [128, 2048], P(('groups', 'seq'), ('tp', 'kv')), parts along dimension 0
There are 2 independent parts, one for each index of `groups`. A program takes and returns all parts, laid end to end along the dimension named above; an argument that names none is the same for every part. Nothing has to cross between parts.
Inputs may be any that keep to these rules, and one draw needn't show every extreme that they name: A user's first 128 * block_counts new events are real; the rest are padding. `semantic_ids`: the codebook entry decoded for each beam row. `beam_parents`: the beam of the previous step that each beam row continues, counted among its user's 16 beams.
All inputs are finite; a program needn't handle non-finite values.
Results may differ from a plain program's by a relative error of at most 0.014.
Values may be sent and summed in bfloat16 or wider, within the bound.
A program may use at most 64 MiB of HBM per device.

v0:
```python
import jax
import jax.numpy as jnp
from jax import lax
from jax.sharding import PartitionSpec as P

H = 16
DH = 128
KVH = 8
BLK = 128
STEPS = 4


eps = 1e-06


def root_norm(values, scale_gain):
    mean_square = jnp.mean(values * values, axis=-1, keepdims=True)
    return values * lax.rsqrt(mean_square + eps) * scale_gain


def shards(
    events,
    history_cache,
    block_counts,
    semantic_ids,
    beam_parents,
    query_weight,
    keyval_weight,
    out_weight,
    cross_weight,
    decoder_query,
    decoder_out,
    code_table,
    encoder_gain,
    cross_gain,
    decoder_gain,
):
    head_size = DH
    group_ratio = H // KVH
    relayed = lax.all_to_all(events, "seq", split_axis=0, concat_axis=1, tiled=True)
    whole = lax.all_gather(relayed, ("tp", "kv"), axis=2, tiled=True)
    users = whole.shape[0]
    length = whole.shape[1]
    width = whole.shape[2]
    source = whole.reshape(users * length, width).astype(jnp.float32)
    normed = root_norm(source, encoder_gain).astype(jnp.bfloat16)
    query_cols = query_weight.shape[1]
    key_cols = keyval_weight.shape[2]
    joined = jnp.concatenate([query_weight, keyval_weight[0], keyval_weight[1]], axis=1)
    projected = jnp.dot(
        normed,
        lax.all_gather(joined, "seq", axis=0, tiled=True),
        preferred_element_type=jnp.float32,
    )
    queries = projected[:, :query_cols].astype(jnp.bfloat16)
    keys_new = projected[:, query_cols : query_cols + key_cols].astype(jnp.bfloat16)
    values_new = projected[:, query_cols + key_cols :].astype(jnp.bfloat16)
    out_full, cross_full = (
        lax.all_gather(out_weight, "seq", axis=0, tiled=True),
        lax.all_gather(cross_weight, "seq", axis=1, tiled=True),
    )
    key_groups = key_cols // head_size
    history_len = history_cache.shape[2]
    query_heads = queries.reshape(users, length, key_groups, group_ratio, head_size)
    key_heads = jnp.concatenate(
        [history_cache[0], keys_new.reshape(users, length, key_cols)], axis=1
    )
    key_heads = key_heads.reshape(users, history_len + length, key_groups, head_size)
    value_heads = jnp.concatenate(
        [history_cache[1], values_new.reshape(users, length, key_cols)], axis=1
    )
    value_heads = value_heads.reshape(users, history_len + length, key_groups, head_size)
    scores = jnp.einsum(
        "uigad,ujgd->ugaij", query_heads, key_heads, preferred_element_type=jnp.float32
    ) * head_size ** (-0.5)
    query_index = lax.broadcasted_iota(jnp.int32, (length, history_len + length), 0)
    key_index = lax.broadcasted_iota(jnp.int32, (length, history_len + length), 1) - history_len
    live_limit = (block_counts * BLK)[:, None, None, None, None]
    visible = (key_index < 0)[None, None, None] | (key_index <= query_index)[None, None, None] & (
        key_index[None, None, None] < live_limit
    )
    raised = jnp.where(visible, jnp.exp(scores), jnp.float32(0.0))
    denominator = jnp.sum(raised, axis=-1, keepdims=True)
    softened = (raised / denominator).astype(jnp.bfloat16)
    attended = jnp.einsum(
        "ugaij,ujgd->uigad", softened, value_heads, preferred_element_type=jnp.float32
    )
    attended = attended.astype(jnp.bfloat16).reshape(users * length, query_cols)
    group = lax.axis_index(("tp", "kv"))
    groups = lax.axis_size(("tp", "kv"))
    share = users * length // groups
    group_term = lax.dot_general(
        attended, out_full, (((1,), (1,)), ((), ())), preferred_element_type=jnp.float32
    ).astype(jnp.bfloat16)
    mixed = lax.psum(group_term, ("tp", "kv")).astype(jnp.float32)
    encoded_all = source + mixed
    cross_all = root_norm(encoded_all, cross_gain).astype(jnp.bfloat16)
    encoded_rows = lax.dynamic_slice_in_dim(encoded_all, group * share, share, 0)
    encoded_out = encoded_rows.astype(jnp.bfloat16).reshape(users, share // users, width)
    cross_keys = jnp.dot(cross_all, cross_full[0], preferred_element_type=jnp.float32).astype(
        jnp.bfloat16
    )
    cross_values = jnp.dot(cross_all, cross_full[1], preferred_element_type=jnp.float32).astype(
        jnp.bfloat16
    )
    cross_key_heads = cross_keys.reshape(users, length, key_groups, head_size)
    cross_value_heads = cross_values.reshape(users, length, key_groups, head_size)
    live_events = (
        lax.broadcasted_iota(jnp.int32, (users, length), 1) < (block_counts * BLK)[:, None]
    )
    live_mask = live_events[:, None, None, None, :]
    beam_rows = semantic_ids.shape[1]
    per_user = beam_rows // users
    vocab_rows = code_table.shape[0]
    vocab_ids = group * vocab_rows + lax.broadcasted_iota(jnp.int32, (1, vocab_rows), 1)

    def lookup(id_values):
        onehot = (id_values[:, None] == vocab_ids).astype(jnp.bfloat16)
        return jnp.dot(onehot, code_table, preferred_element_type=jnp.float32)

    def attend(beam_hidden):
        normed_beams = root_norm(beam_hidden, decoder_gain).astype(jnp.bfloat16)
        beam_queries = jnp.dot(
            normed_beams, decoder_query, preferred_element_type=jnp.float32
        ).astype(jnp.bfloat16)
        beam_queries = beam_queries.reshape(users, per_user, key_groups, group_ratio, head_size)
        beam_scores = jnp.einsum(
            "ubgad,ujgd->ugabj", beam_queries, cross_key_heads, preferred_element_type=jnp.float32
        ) * head_size ** (-0.5)
        beam_raised = jnp.where(live_mask, jnp.exp(beam_scores), jnp.float32(0.0))
        beam_total = jnp.sum(beam_raised, axis=-1, keepdims=True)
        beam_soft = (beam_raised / beam_total).astype(jnp.bfloat16)
        beam_attended = jnp.einsum(
            "ugabj,ujgd->ubgad", beam_soft, cross_value_heads, preferred_element_type=jnp.float32
        )
        beam_attended = beam_attended.astype(jnp.bfloat16).reshape(beam_rows, query_cols)
        return lax.dot_general(
            beam_attended, decoder_out, (((1,), (1,)), ((), ())), preferred_element_type=jnp.float32
        )

    def combine(beam_terms):
        return lax.psum(beam_terms.astype(jnp.bfloat16), ("tp", "kv")).astype(jnp.float32)

    local_rows = lax.broadcasted_iota(jnp.int32, (beam_rows,), 0)
    beam_hidden = combine(lookup(semantic_ids[0]))
    mixed_state = attend(beam_hidden)
    for level in range(1, STEPS):
        source_rows = local_rows // per_user * per_user + beam_parents[level - 1]
        moved = jnp.take(mixed_state, source_rows, axis=0) + lookup(semantic_ids[level])
        beam_hidden = jnp.take(beam_hidden, source_rows, axis=0) + combine(moved)
        mixed_state = attend(beam_hidden)
    finished = (beam_hidden + combine(mixed_state)).astype(jnp.bfloat16)
    width_share = width // groups
    beam_out = lax.dynamic_slice_in_dim(finished, group * width_share, width_share, 1)
    return (encoded_out, beam_out)


def solution(mesh):
    in_specs = (
        P("groups", "seq", ("tp", "kv")),
        P(None, ("groups", "seq"), None, ("tp", "kv")),
        P(("groups", "seq")),
        P(None, ("groups", "seq")),
        P(None, ("groups", "seq")),
        P("seq", ("tp", "kv")),
        P(None, "seq", ("tp", "kv")),
        P("seq", ("tp", "kv")),
        P(None, "seq", ("tp", "kv")),
        P(None, ("tp", "kv")),
        P(None, ("tp", "kv")),
        P(("tp", "kv"), None),
        P(),
        P(),
        P(),
    )
    out_specs = (P(("groups", "seq"), ("tp", "kv"), None), P(("groups", "seq"), ("tp", "kv")))
    return jax.shard_map(shards, mesh=mesh, in_specs=in_specs, out_specs=out_specs, check_vma=False)
```

profile of v0, /device:TPU:0, one launch (start us, length us, event | category | flops | bytes accessed | tf_op | source)
XLA Modules:
  0.0 447.2 jit_solution(481606835040528028)
XLA Ops:
  7.2 21.1 %all_to_all.12 = bf16[4,128,512]{2,1,0:T(8,128)(2,1)} all-to-all(bf16[4,128,512]{2,1,0:T(8,128)(2,1)} %param.17), channel_id=1, replica_groups=mesh['groups'=2,'seq'=4,'tp'=2,'kv'=2] {'seq'}, dimensions={0} | all-to-all | bytes 1048576 | tf_op jit(solution)/shard_map/all_to_all | solution.py:40
  29.5 1.2 pad_maximum_fusion
  34.1 1.6 fusion.15
  35.7 3.5 convolution_convert_fusion.2
  39.2 11.0 %all-gather.5.cloned.1.call-done = bf16[1,512,2048]{2,1,0:T(8,128)(2,1)} async-done(((bf16[1,512,512]{2,1,0:T(8,128)(2,1)}), bf16[1,512,2048]{2,1,0:T(8,128)(2,1)}) %all-gather.5.cloned.1.call-update) | async-done | bytes 2097168 | tf_op jit(solution)/shard_map/all_gather | solution.py:41
  50.2 2.1 fusion.1
  52.3 80.3 %all-gather.7.cloned.1.call-done = bf16[2048,1024]{1,0:T(8,128)(2,1)} async-done(((bf16[512,1024]{1,0:T(8,128)(2,1)}), bf16[2048,1024]{1,0:T(8,128)(2,1)}) %all-gather.7.cloned.1.call-update) | async-done | bytes 4194320 | tf_op jit(solution)/shard_map/all_gather | solution.py:52
  132.5 5.2 %fusion.16 = bf16[512,1024]{1,0:T(8,128)(2,1)S(1)} fusion(bf16[2048,1024]{1,0:T(8,128)(2,1)} %all-gather.7.cloned.1.call-done, bf16[1,512,2048]{2,1,0:T(8,128)(2,1)} %all-gather.5.cloned.1.call-done, f32[2048]{0:T(1024)S(1)} %copy-done.13, f32[512]{0:T(512)S(1)} %add_rsqrt_fusion.1), kind=kOutput, calls=%fused_computation.35 | convolution fusion | flops 2152202240 | bytes 7350272 | tf_op jit(solution)/shard_map/dot_general | solution.py:50
  139.8 3.6 fusion
  143.4 2.4 fusion.19
  145.8 32.5 %all-gather.9.cloned.1.call-done = bf16[2048,512]{1,0:T(8,128)(2,1)} async-done(((bf16[512,512]{1,0:T(8,128)(2,1)}), bf16[2048,512]{1,0:T(8,128)(2,1)}) %all-gather.9.cloned.1.call-update) | async-done | bytes 2097168 | tf_op jit(solution)/shard_map/all_gather | solution.py:59
  178.3 4.2 convolution_convert_fusion
  183.4 50.6 %all-reduce.15.cloned.1.call-done = (bf16[512,2048]{1,0:T(8,128)(2,1)}, bf16[16,2048]{1,0:T(8,128)(2,1)}) async-done(((bf16[512,2048]{1,0:T(8,128)(2,1)}, bf16[16,2048]{1,0:T(8,128)(2,1)}), (bf16[512,2048]{1,0:T(8,128)(2,1)}, bf16[16,2048]{1,0:T(8,128)(2,1)})) %all-reduce.15.cloned.1.call-update) | async-done | bytes 2162704 | tf_op jit(solution)/shard_map/psum | solution.py:95
  235.0 2.1 convolution_convert_fusion.12
  237.0 3.0 multiply_reduce_fusion
  240.0 41.1 %all-gather.11.cloned.1.call-done = bf16[2,2048,256]{2,1,0:T(8,128)(2,1)} async-done(((bf16[2,512,256]{2,1,0:T(8,128)(2,1)}), bf16[2,2048,256]{2,1,0:T(8,128)(2,1)}) %all-gather.11.cloned.1.call-update) | async-done | bytes 2097168 | tf_op jit(solution)/shard_map/all_gather | solution.py:60
  281.2 3.8 convolution_convert_fusion.3
  285.6 1.2 convolution_convert_fusion.4
  288.3 3.5 fusion.6
  292.6 29.8 %all-reduce.7.cloned.1.call-done = bf16[16,2048]{1,0:T(8,128)(2,1)} async-done(((bf16[16,2048]{1,0:T(8,128)(2,1)}), bf16[16,2048]{1,0:T(8,128)(2,1)}) %all-reduce.7.cloned.1.call-update) | async-done | bytes 65552 | tf_op jit(solution)/shard_map/psum | solution.py:142
  323.5 2.0 convolution_convert_fusion.10
  327.3 3.5 fusion.7
  331.5 31.0 %all-reduce.9.cloned.1.call-done = bf16[16,2048]{1,0:T(8,128)(2,1)} async-done(((bf16[16,2048]{1,0:T(8,128)(2,1)}), bf16[16,2048]{1,0:T(8,128)(2,1)}) %all-reduce.9.cloned.1.call-update) | async-done | bytes 65552 | tf_op jit(solution)/shard_map/psum | solution.py:142
  363.6 2.0 convolution_convert_fusion.8
  367.4 3.5 fusion.8
  371.0 4.4 convert_add_fusion
  376.1 26.6 %all-reduce.11.cloned.1.call-done = bf16[16,2048]{1,0:T(8,128)(2,1)} async-done(((bf16[16,2048]{1,0:T(8,128)(2,1)}), bf16[16,2048]{1,0:T(8,128)(2,1)}) %all-reduce.11.cloned.1.call-update) | async-done | bytes 65552 | tf_op jit(solution)/shard_map/psum | solution.py:142
  403.7 2.0 convolution_convert_fusion.6
  406.3 1.3 convolution_convert_fusion.1
  407.6 1.9 fusion.42
  409.5 29.8 %all-reduce.13.cloned.1.call-done = bf16[16,2048]{1,0:T(8,128)(2,1)} async-done(((bf16[16,2048]{1,0:T(8,128)(2,1)}), bf16[16,2048]{1,0:T(8,128)(2,1)}) %all-reduce.13.cloned.1.call-update) | async-done | bytes 65552 | tf_op jit(solution)/shard_map/psum | solution.py:142
  439.3 1.3 fusion.66
  (108 shorter events, 19.2 us)
Async XLA Ops:
  7.2 279.9 %copy-start = (bf16[2048,512]{1,0:T(8,128)(2,1)S(1)}, bf16[2048,512]{1,0:T(8,128)(2,1)}, u32[]{:S(2)}) copy-start(bf16[2048,512]{1,0:T(8,128)(2,1)} %param.27) | copy-start | bytes 6291460
  7.2 22.3 %copy-start.6 = (bf16[512,512]{1,0:T(8,128)(2,1)S(1)}, bf16[512,512]{1,0:T(8,128)(2,1)}, u32[]{:S(2)}) copy-start(bf16[512,512]{1,0:T(8,128)(2,1)} %param.22) | copy-start | bytes 1572868
  7.2 43.0 %all-gather.5.cloned.1.call-start = ((), (), s32[]{:S(2)}) async-start(), calls=%async_computation.1 | async-start | bytes 2621440 | tf_op jit(solution)/shard_map/all_gather | solution.py:41
  28.3 104.2 %all-gather.7.cloned.1.call-start = ((), (), s32[]{:S(2)}) async-start(), calls=%async_computation.2 | async-start | bytes 5242880 | tf_op jit(solution)/shard_map/all_gather | solution.py:52
  29.5 2.7 copy-start.4
  30.7 3.4 copy-start.10
  30.7 147.6 %all-gather.9.cloned.1.call-start = ((), (), s32[]{:S(2)}) async-start(), calls=%async_computation.3 | async-start | bytes 2621440 | tf_op jit(solution)/shard_map/all_gather | solution.py:59
  31.5 202.5 %all-reduce.15.cloned.1.call-start = ((), (), s32[]{:S(2)}) async-start(), calls=%async_computation.9 | async-start | bytes 4325376 | tf_op jit(solution)/shard_map/psum | solution.py:95
  39.2 93.3 %copy-start.13 = (f32[2048]{0:T(1024)S(1)}, f32[2048]{0:T(1024)}, u32[]{:S(2)}) copy-start(f32[2048]{0:T(1024)} %param.29) | copy-start | bytes 24580
  137.9 1.9 copy-start.8
  139.8 3.6 copy-start.5
  139.8 3.6 copy-start.7
  182.5 0.9 copy-start.11
  182.5 52.4 %copy-start.9 = (f32[2048]{0:T(1024)S(1)}, f32[2048]{0:T(1024)}, u32[]{:S(2)}) copy-start(f32[2048]{0:T(1024)} %param.31) | copy-start | bytes 24580
  182.5 98.6 %all-gather.11.cloned.1.call-start = ((), (), s32[]{:S(2)}) async-start(), calls=%async_computation.4 | async-start | bytes 2621440 | tf_op jit(solution)/shard_map/all_gather | solution.py:60
  183.1 139.3 %all-reduce.7.cloned.1.call-start = ((), (), s32[]{:S(2)}) async-start(), calls=%async_computation.5 | async-start | bytes 131072 | tf_op jit(solution)/shard_map/psum | solution.py:142
  237.0 44.1 %copy-start.14 = (f32[2048]{0:T(1024)S(1)}, f32[2048]{0:T(1024)}, u32[]{:S(2)}) copy-start(f32[2048]{0:T(1024)} %param.30) | copy-start | bytes 24580
  281.2 4.0 copy-start.1
  281.2 4.0 copy-start.2
  281.2 4.4 copy-start.12
  288.3 3.6 copy-start.3
  291.9 70.6 %all-reduce.9.cloned.1.call-start = ((), (), s32[]{:S(2)}) async-start(), calls=%async_computation.6 | async-start | bytes 131072 | tf_op jit(solution)/shard_map/psum | solution.py:142
  330.8 71.8 %all-reduce.11.cloned.1.call-start = ((), (), s32[]{:S(2)}) async-start(), calls=%async_computation.7 | async-start | bytes 131072 | tf_op jit(solution)/shard_map/psum | solution.py:142
  371.0 68.3 %all-reduce.13.cloned.1.call-start = ((), (), s32[]{:S(2)}) async-start(), calls=%async_computation.8 | async-start | bytes 131072 | tf_op jit(solution)/shard_map/psum | solution.py:142
Sparse Core Ops, SparseCore 0:
  28.5 21.6 all-gather.4
  51.8 80.7 all-gather.6
  134.1 44.1 all-gather.8
  182.7 51.2 all-reduce.14
  235.4 45.7 all-gather.10
  292.0 30.3 all-reduce.6
  331.0 31.5 all-reduce.8
  371.1 31.5 all-reduce.10
  407.7 31.5 all-reduce.12
where the time goes:
time: 448 us; the launch traced here: 447 us
  waiting for transfers between devices  334 us (75%)
  matrix products  47.6 us (11%)
  blocking collectives  21.1 us (5%)
  other arithmetic  17.9 us (4%)
  between operations  14.9 us (3%)
  local copies, waits for them, and re-layouts  11.2 us (2%)
    psum x4, waiting for transfers between devices, combine(): lax.psum(beam_terms.astype(jnp.bfloat16), ('tp', 'kv')).astype(jnp.float32)  117 us
    all_gather x1, waiting for transfers between devices, shards(): lax.all_gather(joined, 'seq', axis=0, tiled=True)  80.3 us
    psum x1, waiting for transfers between devices, shards(): mixed = lax.psum(group_term, ('tp', 'kv')).astype(jnp.float32)  50.6 us
    all_gather x1, waiting for transfers between devices, shards(): lax.all_gather(cross_weight, 'seq', axis=1, tiled=True)  41.1 us
    all_gather x1, waiting for transfers between devices, shards(): lax.all_gather(out_weight, 'seq', axis=0, tiled=True)  32.5 us
    all_to_all x1, blocking collectives, shards(): lax.all_to_all(events, 'seq', split_axis=0, concat_axis=1, tiled=True)  21.1 us
    dot_general x4, matrix products, lookup(): return jnp.dot(onehot, code_table, preferred_element_type=jnp.float32)  14.1 us
    all_gather x1, waiting for transfers between devices, shards(): whole = lax.all_gather(relayed, ('tp', 'kv'), axis=2, tiled=True)  11 us
  transfers between devices with their start and end apart: 9, of which 9 were waited for; matrix products, arithmetic and copies ran while one was open for 9% of the time, Pallas kernels for 0%

commit v1 on v0

v1 whole, which is shorter than its diff:
```python
import functools

import jax
import jax.numpy as jnp
from jax import lax
from jax.experimental import pallas as pl
from jax.experimental.pallas import tpu as pltpu
from jax.sharding import PartitionSpec as P

DH = 128
BLK = 128
eps = 1e-06
F32 = jnp.float32
BF16 = jnp.bfloat16
MESH = pl.DeviceIdType.MESH


def unit(values):
    return lax.rsqrt(jnp.mean(values * values, axis=-1, keepdims=True) + eps)


def dot(a, b):
    return jnp.dot(a, b, preferred_element_type=F32)


def dot_t(a, b):
    return lax.dot_general(a, b, (((1,), (1,)), ((), ())), preferred_element_type=F32)


def body(
    sizes,
    events, history, counts, ids, parents, wq_in, wkv_in, wo_in, wc_in, dq_in, do_in, table_in,
    egain, cgain, dgain,
    enc_out, beam_out,
    wq, wkv, wo, wc, dq, do, table, hist, xb, normed, qs, kn, vn, att, gterm, rk, s1, rt, cx, ck, cv,
    look, terms, last_own, last_in, hidden_ref, mixed_ref, ba,
    local_sem, z_send, z_recv, y_send, y_recv, ev_send, ev_recv,
    ag_send, ag_recv, lk_send, lk_recv, rk_send, rk_recv, rt_send, rt_recv, tm_send, tm_recv,
):
    G, S, T, K = sizes
    TK = T * K
    g, s = lax.axis_index("groups"), lax.axis_index("seq")
    t, k = lax.axis_index("tp"), lax.axis_index("kv")
    p = t * K + k
    rows = wq_in.shape[0]
    part = rows // G
    width = wq.shape[0]
    length = normed.shape[0]
    block = length // S
    share = length // TK
    cols = wq.shape[1]
    kcols = kn.shape[1]
    beams = hidden_ref.shape[0]
    steps = ids.shape[0] // beams
    pending = []

    def when(condition, action):
        if condition is True:
            action()
        else:
            pl.when(condition)(action)

    def send(make, condition=True):
        when(condition, lambda: make().start())
        pending.append((make, condition))

    def remote(src, dst, ss, rs, **where):
        return pltpu.make_async_remote_copy(
            src_ref=src, dst_ref=dst, send_sem=ss, recv_sem=rs, device_id=where, device_id_type=MESH
        )

    barrier = pltpu.get_barrier_semaphore()
    for j in range(1, S):
        pl.semaphore_signal(barrier, inc=1, device_id={"seq": lax.rem(s + j, S)}, device_id_type=MESH)
    for j in range(1, G):
        pl.semaphore_signal(barrier, inc=1, device_id={"groups": lax.rem(g + j, G)}, device_id_type=MESH)
    peers = []
    for j in range(1, TK):
        other = lax.rem(p + j, TK)
        peers.append((j - 1, other, lax.div(other, K), lax.rem(other, K)))
        pl.semaphore_signal(
            barrier, inc=1, device_id={"tp": peers[-1][2], "kv": peers[-1][3]}, device_id_type=MESH
        )

    mine = pl.ds(pl.multiple_of(s * rows, rows), rows)
    stay = pl.ds(pl.multiple_of(s * block, block), block)
    local = [
        pltpu.make_async_copy(a, b, local_sem.at[i])
        for i, (a, b) in enumerate(
            [
                (events.at[s], xb.at[p, stay]),
                (wq_in, wq.at[mine]),
                (wkv_in, wkv.at[:, mine]),
                (table_in, table),
                (history.at[:, 0], hist),
                (wo_in, wo.at[mine]),
                (wc_in, wc.at[:, mine]),
                (dq_in, dq),
                (do_in, do),
            ]
        )
    ]
    for copy in local:
        copy.start()
    pl.semaphore_wait(barrier, (S - 1) + (G - 1) + (TK - 1))

    for j in range(1, S):

        def make(j=j):
            to = lax.rem(s + j, S)
            return remote(
                events.at[to], xb.at[p, stay], ev_send.at[j - 1], ev_recv.at[j - 1], seq=to
            )

        send(make)

    def at(array, origin, which):
        where = pl.ds(pl.multiple_of(origin * rows + which * part, part), part)
        return [wq, wo][array == 2].at[where] if array in (0, 2) else [wkv, wc][array == 3].at[:, where]

    def own(array):
        where = pl.ds(pl.multiple_of(g * part, part), part)
        source = [wq_in, wkv_in, wo_in, wc_in][array]
        return source.at[where] if array in (0, 2) else source.at[:, where]

    def hop(array, side, r):
        step = 1 if side == 0 else -1

        def make():
            origin = s - step * r
            src = own(array) if r == 0 else at(array, origin, g)
            return remote(
                src, at(array, origin, g), z_send.at[array, side, r], z_recv.at[array, side, r], seq=s + step
            )

        ok = s + step < S if side == 0 else s + step >= 0
        if r > 0:
            ok = jnp.logical_and(ok, s - r >= 0 if side == 0 else s + r < S)
        send(make, ok)

    def across(array, side, r):
        step = 1 if side == 0 else -1
        ok = s - r >= 0 if side == 0 else s + r < S
        for j in range(1, G):

            def make(j=j):
                piece = at(array, s - step * r, g)
                return remote(
                    piece, piece, y_send.at[array, side, r, j - 1], y_recv.at[array, side, r, j - 1],
                    groups=lax.rem(g + j, G),
                )

            send(make, ok)

    def arrive(array, r):
        for side in (0, 1):
            step = 1 if side == 0 else -1
            ok = s - r >= 0 if side == 0 else s + r < S

            def wait(side=side, step=step):
                piece = at(array, s - step * r, g)
                remote(
                    piece, piece, z_send.at[array, side, r - 1], z_recv.at[array, side, r - 1], seq=s
                ).wait_recv()

            when(ok, wait)
            if r + 1 < S:
                hop(array, side, r)
            across(array, side, r)

    def settle(array):
        for r in range(1, S):
            for side in (0, 1):
                step = 1 if side == 0 else -1
                ok = s - r >= 0 if side == 0 else s + r < S

                def wait(side=side, step=step, r=r):
                    for j in range(1, G):
                        piece = at(array, s - step * r, lax.rem(g - j + G, G))
                        remote(
                            piece, piece, y_send.at[array, side, r, j - 1], y_recv.at[array, side, r, j - 1],
                            groups=g,
                        ).wait_recv()

                when(ok, wait)

    def begin(array):
        hop(array, 0, 0)
        hop(array, 1, 0)

    begin(0)
    begin(1)

    def spread(buffer, base):
        def give(source, slot, **where):
            def make():
                piece = buffer.at[source]
                return remote(piece, piece, ag_send.at[slot], ag_recv.at[slot], **where)

            send(make)

        def take(source, slot):
            piece = buffer.at[source]
            remote(piece, piece, ag_send.at[slot], ag_recv.at[slot], tp=t).wait_recv()

        for i in range(1, T):
            give(p, base + i, tp=lax.rem(t + i, T))
        for j in range(1, K):
            give(p, base + T * j, kv=lax.rem(k + j, K))

        def relay():
            for i in range(1, T):
                there = lax.rem(t - i + T, T) * K + k
                take(there, base + i)
                for j in range(1, K):
                    give(there, base + T * j + i, kv=lax.rem(k + j, K))

        def finish():
            for j in range(1, K):
                for i in range(T):
                    there = lax.rem(t - i + T, T) * K + lax.rem(k - j + K, K)
                    take(there, base + T * j + i)

        return relay, finish

    local[0].wait()
    for j in range(1, S):
        came = pl.ds(pl.multiple_of(lax.rem(s - j + S, S) * block, block), block)
        piece = xb.at[p, came]
        remote(piece, piece, ev_send.at[j - 1], ev_recv.at[j - 1], seq=s).wait_recv()
    relay, finish = spread(xb, 0)

    local[3].wait()
    vocab = table.shape[0]
    onehot = (
        ids[...] == p * vocab + lax.broadcasted_iota(jnp.int32, (ids.shape[0], vocab), 1)
    ).astype(BF16)
    for c in range(TK):
        span = slice(c * cols, (c + 1) * cols)
        look[p, :, span] = dot(onehot, table[:, span]).astype(BF16)

    arrive(0, 1)
    arrive(1, 1)
    relay()
    for slot, other, pt, pk in peers:

        def make(slot=slot, pt=pt, pk=pk):
            return remote(look.at[p], look.at[p], lk_send.at[slot], lk_recv.at[slot], tp=pt, kv=pk)

        send(make)
    finish()
    for c in range(S):
        lines = slice(c * block, (c + 1) * block)
        source = [xb[q, lines].astype(F32) for q in range(TK)]
        square = sum(jnp.sum(v * v, axis=-1, keepdims=True) for v in source)
        scale = lax.rsqrt(square / width + eps)
        for q in range(TK):
            span = slice(q * cols, (q + 1) * cols)
            normed[lines, span] = (source[q] * scale * egain[:, span]).astype(BF16)
    for r in range(2, S):
        arrive(0, r)
        arrive(1, r)
    begin(2)
    begin(3)
    for i in (1, 2, 4):
        local[i].wait()
    settle(0)
    settle(1)

    qs[...] = dot(normed[...], wq[...]).astype(BF16)
    kn[...] = dot(normed[...], wkv[0]).astype(BF16)
    vn[...] = dot(normed[...], wkv[1]).astype(BF16)

    heads = cols // DH
    ratio = cols // kcols
    limit = counts[0] * BLK
    chunk = min(128, length)
    turns = [(a, r) for r in range(1, S) for a in (2, 3)]
    spots = heads * (length // chunk)
    done = 0
    spot = 0
    for h in range(heads):
        hs = slice(h * DH, (h + 1) * DH)
        ks = slice(h // ratio * DH, (h // ratio + 1) * DH)
        for c in range(length // chunk):
            lines = slice(c * chunk, (c + 1) * chunk)
            reach = (c + 1) * chunk
            q = qs[lines, hs]
            old = jnp.exp(dot_t(q, hist[0, :, ks]) * DH ** (-0.5))
            new = jnp.exp(dot_t(q, kn[:reach, ks]) * DH ** (-0.5))
            qi = lax.broadcasted_iota(jnp.int32, (chunk, reach), 0) + c * chunk
            ki = lax.broadcasted_iota(jnp.int32, (chunk, reach), 1)
            new = jnp.where((ki <= qi) & (ki < limit), new, 0.0)
            total = jnp.sum(old, axis=-1, keepdims=True) + jnp.sum(new, axis=-1, keepdims=True)
            att[lines, hs] = (
                dot((old / total).astype(BF16), hist[1, :, ks])
                + dot((new / total).astype(BF16), vn[:reach, ks])
            ).astype(BF16)
            spot += 1
            while done * spots < (spot - spots // 4) * len(turns):
                arrive(*turns[done])
                done += 1
    while done < len(turns):
        arrive(*turns[done])
        done += 1
    local[5].wait()
    settle(2)

    def project(which):
        lines = pl.ds(pl.multiple_of(which * share, share), share)
        for c in range(TK):
            span = slice(c * cols, (c + 1) * cols)
            gterm[which, :, span] = dot_t(att[lines, :], wo[span, :]).astype(BF16)

    for j in range(1, K):
        pk = lax.rem(k + j, K)
        for i in range(T):
            it = lax.rem(t + 1 + i, T)
            project(it * K + pk)

            def make(j=j, i=i, pk=pk, it=it):
                return remote(
                    gterm.at[it * K + pk], rk.at[j - 1, i], rk_send.at[j - 1, i], rk_recv.at[j - 1, i], kv=pk
                )

            send(make)
    for i in range(T):
        project(lax.rem(t + 1 + i, T) * K + k)
    total = None
    for i in range(T):
        for j in range(1, K):
            piece = rk.at[j - 1, i]
            remote(piece, piece, rk_send.at[j - 1, i], rk_recv.at[j - 1, i], kv=k).wait_recv()
        it = lax.rem(t + 1 + i, T)
        total = gterm[it * K + k].astype(F32)
        for j in range(1, K):
            total = total + rk[j - 1, i].astype(F32)
        if i < T - 1:
            s1[i] = total.astype(BF16)

            def make(i=i, it=it):
                return remote(s1.at[i], rt.at[i], rt_send.at[i], rt_recv.at[i], tp=it)

            send(make)
        else:
            mixed_ref[...] = total
    for i in range(T - 1):
        remote(rt.at[i], rt.at[i], rt_send.at[i], rt_recv.at[i], tp=t).wait_recv()
    total = mixed_ref[...]
    for i in range(T - 1):
        total = total + rt[i].astype(F32)
    mine = pl.ds(pl.multiple_of(p * share, share), share)
    mixed_ref[...] = total
    square = jnp.zeros((share, 1), F32)
    for q in range(TK):
        span = slice(q * cols, (q + 1) * cols)
        value = mixed_ref[:, span] + xb[q, mine].astype(F32)
        mixed_ref[:, span] = value
        square = square + jnp.sum(value * value, axis=-1, keepdims=True)
        enc_out[:, span] = value.astype(BF16)
    scale = lax.rsqrt(square / width + eps)
    cx[p] = (mixed_ref[...] * scale * cgain[...]).astype(BF16)
    relay, finish = spread(cx, TK)

    local[7].wait()
    local[8].wait()
    for slot, other, pt, pk in peers:
        piece = look.at[lax.rem(p - slot - 1 + TK, TK)]
        remote(piece, piece, lk_send.at[slot], lk_recv.at[slot], tp=t).wait_recv()

    def code(level):
        lines = slice(level * beams, (level + 1) * beams)
        return sum(look[q, lines].astype(F32) for q in range(TK))

    def query():
        hidden = hidden_ref[...]
        return dot((hidden * unit(hidden) * dgain[...]).astype(BF16), dq[...]).astype(BF16)

    hidden_ref[...] = code(0)
    queries = query()
    relay()
    local[6].wait()
    settle(3)
    finish()
    for q in range(TK):
        lines = slice(q * share, (q + 1) * share)
        ck[lines] = dot(cx[q], wc[0]).astype(BF16)
        cv[lines] = dot(cx[q], wc[1]).astype(BF16)

    live = lax.broadcasted_iota(jnp.int32, (ratio * beams, length), 1) < limit
    for level in range(steps):
        for j in range(kcols // DH):
            ks = slice(j * DH, (j + 1) * DH)
            q = jnp.concatenate(
                [queries[:, (j * ratio + a) * DH : (j * ratio + a + 1) * DH] for a in range(ratio)], axis=0
            )
            raised = jnp.where(live, jnp.exp(dot_t(q, ck[:, ks]) * DH ** (-0.5)), 0.0)
            soft = (raised / jnp.sum(raised, axis=-1, keepdims=True)).astype(BF16)
            found = dot(soft, cv[:, ks]).astype(BF16)
            for a in range(ratio):
                h = j * ratio + a
                ba[:, h * DH : (h + 1) * DH] = found[a * beams : (a + 1) * beams]
        if level < steps - 1:
            for c in range(TK):
                span = slice(c * cols, (c + 1) * cols)
                terms[level, p, :, span] = dot_t(ba[...], do[span, :]).astype(BF16)
            for slot, other, pt, pk in peers:

                def make(slot=slot, pt=pt, pk=pk, level=level):
                    piece = terms.at[level, p]
                    return remote(
                        piece, piece, tm_send.at[level, slot], tm_recv.at[level, slot], tp=pt, kv=pk
                    )

                send(make)
            lines = slice(level * beams, (level + 1) * beams)
            pick = (
                parents[lines, :] == lax.broadcasted_iota(jnp.int32, (beams, beams), 1)
            ).astype(F32)
            nextcode = code(level + 1)
            for slot, other, pt, pk in peers:
                piece = terms.at[level, lax.rem(p - slot - 1 + TK, TK)]
                remote(piece, piece, tm_send.at[level, slot], tm_recv.at[level, slot], tp=t).wait_recv()
            state = hidden_ref[...] + sum(terms[level, q].astype(F32) for q in range(TK))
            moved = jnp.dot(pick, state, preferred_element_type=F32, precision=lax.Precision.HIGHEST)
            hidden_ref[...] = moved + nextcode
            queries = query()
        else:
            for c in range(TK):
                span = slice(c * cols, (c + 1) * cols)
                term = dot_t(ba[...], do[span, :])
                last_own[c] = term.astype(BF16)
            for slot, other, pt, pk in peers:

                def make(slot=slot, other=other, pt=pt, pk=pk, level=level):
                    return remote(
                        last_own.at[other], last_in.at[slot],
                        tm_send.at[level, slot], tm_recv.at[level, slot], tp=pt, kv=pk,
                    )

                send(make)
            value = jnp.zeros((beams, cols), F32)
            for c in range(TK):
                span = slice(c * cols, (c + 1) * cols)
                value = jnp.where(p == c, hidden_ref[:, span], value)
            value = value + last_own[p].astype(F32)
            for slot, other, pt, pk in peers:
                piece = last_in.at[slot]
                remote(piece, piece, tm_send.at[level, slot], tm_recv.at[level, slot], tp=t).wait_recv()
            for slot in range(TK - 1):
                value = value + last_in[slot].astype(F32)
            beam_out[...] = value.astype(BF16)

    for make, condition in pending:
        when(condition, lambda make=make: make().wait_send())


def solution(mesh):
    G, S, T, K = (mesh.shape[a] for a in ("groups", "seq", "tp", "kv"))
    TK = T * K

    def shards(
        events, history, counts, ids, parents, wq, wkv, wo, wc, dq, do, table, egain, cgain, dgain
    ):
        users, block, cols = events.shape
        length = block * S
        share = length // TK
        rows, kcols = wkv.shape[1:]
        width = rows * S
        steps, beams = ids.shape
        hist_len = history.shape[2]
        vm = lambda *shape: pltpu.VMEM(shape, BF16)
        vf = lambda *shape: pltpu.VMEM(shape, F32)
        dma = lambda *shape: pltpu.SemaphoreType.DMA(shape)
        anywhere = pl.BlockSpec(memory_space=pl.ANY)
        vmem = pl.BlockSpec(memory_space=pltpu.VMEM)
        smem = pl.BlockSpec(memory_space=pltpu.SMEM)
        enc, beam = pl.pallas_call(
            functools.partial(body, (G, S, T, K)),
            out_shape=(
                jax.ShapeDtypeStruct((share, width), BF16),
                jax.ShapeDtypeStruct((beams, cols), BF16),
            ),
            in_specs=[anywhere, anywhere, smem, vmem, vmem] + [anywhere] * 7 + [vmem] * 3,
            out_specs=(vmem, vmem),
            scratch_shapes=[
                vm(width, cols), vm(2, width, kcols), vm(width, cols), vm(2, width, kcols),
                vm(width, cols), vm(width, cols), vm(*table.shape), vm(2, hist_len, kcols),
                vm(TK, length, cols), vm(length, width),
                vm(length, cols), vm(length, kcols), vm(length, kcols), vm(length, cols),
                vm(TK, share, width), vm(max(K - 1, 1), T, share, width), vm(max(T - 1, 1), share, width),
                vm(max(T - 1, 1), share, width), vm(TK, share, width), vm(length, kcols), vm(length, kcols),
                vm(TK, steps * beams, width), vm(steps, TK, beams, width),
                vm(TK, beams, cols), vm(TK, beams, cols),
                vf(beams, width), vf(share, width), vm(beams, cols),
                dma(9), dma(4, 2, S), dma(4, 2, S), dma(4, 2, S, G), dma(4, 2, S, G), dma(S), dma(S),
                dma(2 * TK), dma(2 * TK), dma(TK), dma(TK), dma(K, T), dma(K, T), dma(T), dma(T),
                dma(steps, TK), dma(steps, TK),
            ],
            compiler_params=pltpu.CompilerParams(
                collective_id=0, has_side_effects=True, vmem_limit_bytes=60 * 1024 * 1024
            ),
        )(
            events, history, counts, ids.reshape(-1, 1), parents.reshape(-1, 1), wq, wkv, wo, wc, dq, do,
            table, egain[None], cgain[None], dgain[None],
        )
        return enc[None], beam

    in_specs = (
        P("groups", "seq", ("tp", "kv")),
        P(None, ("groups", "seq"), None, ("tp", "kv")),
        P(("groups", "seq")),
        P(None, ("groups", "seq")),
        P(None, ("groups", "seq")),
        P("seq", ("tp", "kv")),
        P(None, "seq", ("tp", "kv")),
        P("seq", ("tp", "kv")),
        P(None, "seq", ("tp", "kv")),
        P(None, ("tp", "kv")),
        P(None, ("tp", "kv")),
        P(("tp", "kv"), None),
        P(),
        P(),
        P(),
    )
    out_specs = (P(("groups", "seq"), ("tp", "kv"), None), P(("groups", "seq"), ("tp", "kv")))
    return jax.shard_map(shards, mesh=mesh, in_specs=in_specs, out_specs=out_specs, check_vma=False)
```

time: 448 us -> 154 us (0.34)
  waiting for transfers between devices: 334 us -> 0 us
  Pallas kernels: 0 us -> 147 us
  matrix products: 47.6 us -> 0 us
  blocking collectives: 21.1 us -> 0 us
  other arithmetic: 17.9 us -> 0 us
  between operations: 14.9 us -> 1.29 us
  local copies, waits for them, and re-layouts: 11.2 us -> 5.97 us
    psum x5 -> x0, waiting for transfers between devices: 168 us -> none  [the longest x4 117 us: combine(): lax.psum(beam_terms.astype(jnp.bfloat16), ('tp', 'kv')).astype(jnp.float32)]
    all_gather x4 -> x0, waiting for transfers between devices: 165 us -> none  [the longest x1 80.3 us: shards(): lax.all_gather(joined, 'seq', axis=0, tiled=True)]
    pallas_call x0 -> x1, Pallas kernels: none -> 147 us  [shards(): pl.pallas_call(functools.partial(body, (G, S, T, K)), out_shape=(jax.Shap...]
    dot_general x26 -> x0, matrix products: 47.6 us -> none  [the longest x4 14.1 us: lookup(): return jnp.dot(onehot, code_table, preferred_element_type=jnp.float32)]
    all_to_all x1 -> x0, blocking collectives: 21.1 us -> none  [shards(): lax.all_to_all(events, 'seq', split_axis=0, concat_axis=1, tiled=True)]
    reduce_sum x6 -> x0, other arithmetic: 9.15 us -> none  [root_norm(): mean_square = jnp.mean(values * values, axis=-1, keepdims=True)]
  transfers between devices with their start and end apart: 9 -> 0, of which waited for: 9 -> 0; matrix products, arithmetic and copies ran while one was open for 9% -> 0% of each run, Pallas kernels for 0% -> 0%
where the time goes in v1:
time: 154 us
  Pallas kernels  147 us (95%)
  local copies, waits for them, and re-layouts  5.97 us (4%)
    pallas_call x1, Pallas kernels, shards(): pl.pallas_call(functools.partial(body, (G, S, T, K)), out_shape=(jax.Shap...  147 us
    unnamed x2, local copies, waits for them, and re-layouts  3.2 us

profile of v1, /device:TPU:0, one launch (start us, length us, event | category | flops | bytes accessed | tf_op | source)
XLA Modules:
  0.0 153.9 jit_solution(2589970995520060572)
XLA Ops:
  1.3 1.4 reshape.13.parents
  2.7 1.4 reshape.12.ids
  4.0 146.6 %shard_map.158 = (bf16[128,2048]{1,0:T(8,128)(2,1)}, bf16[16,512]{1,0:T(8,128)(2,1)}) custom-call(bf16[4,128,512]{2,1,0:T(8,128)(2,1)} %events.1, bf16[2,1,512,256]{3,2,1,0:T(8,128)(2,1)} %history.1, s32[1]{0:T(128)S(6)} %copy.21.counts, s32[64,1]{1,0:T(8,128)} %reshape.12.ids, s32[48,1]{1,0:T(8,128)} %reshape.13.parents, bf16[512,512]{1,0:T(8,128)(2,1)} %wq_in.1, ...), custom_call_target="tpu_custom_call" | custom-call | tf_op jit(solution)/shard_map/pallas_call | solution.py:478
  150.7 1.9 %copy.22 = bf16[1,128,2048]{2,1,0:T(8,128)(2,1)} copy(bf16[1,128,2048]{2,1,0:T(8,128)(2,1)} %bitcast.4) | data formatting | bytes 1048576
  152.6 1.3 copy.23

commit v2 on v1

--- a/solution.py
+++ b/solution.py
@@ -33,7 +33,7 @@
     egain, cgain, dgain,
     enc_out, beam_out,
     wq, wkv, wo, wc, dq, do, table, hist, xb, normed, qs, kn, vn, att, gterm, rk, s1, rt, cx, ck, cv,
-    look, terms, last_own, last_in, hidden_ref, mixed_ref, ba,
+    look, terms, last_own, last_in, hidden_ref, mixed_ref, ba, old,
     local_sem, z_send, z_recv, y_send, y_recv, ev_send, ev_recv,
     ag_send, ag_recv, lk_send, lk_recv, rk_send, rk_recv, rt_send, rt_recv, tm_send, tm_recv,
 ):
@@ -51,7 +51,7 @@
     cols = wq.shape[1]
     kcols = kn.shape[1]
     beams = hidden_ref.shape[0]
-    steps = ids.shape[0] // beams
+    steps = ids.shape[0]
     pending = []
 
     def when(condition, action):
@@ -114,14 +114,27 @@
 
         send(make)
 
+    arrays = [
+        (wq, wq_in, None, 0, 2), (wq, wq_in, None, 1, 2),
+        (wkv, wkv_in, 0, 0, 1), (wkv, wkv_in, 1, 0, 1),
+        (wo, wo_in, None, 0, 2), (wo, wo_in, None, 1, 2),
+        (wc, wc_in, slice(None), 0, 1),
+    ]
+
+    def cut(ref, array, start):
+        lead, sub, of = arrays[array][2:]
+        size = part // of
+        where = pl.ds(pl.multiple_of(start + sub * size, size), size)
+        return ref.at[where] if lead is None else ref.at[lead, where]
+
     def at(array, origin, which):
-        where = pl.ds(pl.multiple_of(origin * rows + which * part, part), part)
-        return [wq, wo][array == 2].at[where] if array in (0, 2) else [wkv, wc][array == 3].at[:, where]
+        return cut(arrays[array][0], array, origin * rows + which * part)
 
     def own(array):
-        where = pl.ds(pl.multiple_of(g * part, part), part)
-        source = [wq_in, wkv_in, wo_in, wc_in][array]
-        return source.at[where] if array in (0, 2) else source.at[:, where]
+        return cut(arrays[array][1], array, g * part)
+
+    def there(side, r):
+        return s - r >= 0 if side == 0 else s + r < S
 
     def hop(array, side, r):
         step = 1 if side == 0 else -1
@@ -135,12 +148,11 @@
 
         ok = s + step < S if side == 0 else s + step >= 0
         if r > 0:
-            ok = jnp.logical_and(ok, s - r >= 0 if side == 0 else s + r < S)
+            ok = jnp.logical_and(ok, there(side, r))
         send(make, ok)
 
     def across(array, side, r):
         step = 1 if side == 0 else -1
-        ok = s - r >= 0 if side == 0 else s + r < S
         for j in range(1, G):
 
             def make(j=j):
@@ -150,12 +162,11 @@
                     groups=lax.rem(g + j, G),
                 )
 
-            send(make, ok)
+            send(make, there(side, r))
 
     def arrive(array, r):
         for side in (0, 1):
             step = 1 if side == 0 else -1
-            ok = s - r >= 0 if side == 0 else s + r < S
 
             def wait(side=side, step=step):
                 piece = at(array, s - step * r, g)
@@ -163,7 +174,7 @@
                     piece, piece, z_send.at[array, side, r - 1], z_recv.at[array, side, r - 1], seq=s
                 ).wait_recv()
 
-            when(ok, wait)
+            when(there(side, r), wait)
             if r + 1 < S:
                 hop(array, side, r)
             across(array, side, r)
@@ -172,7 +183,6 @@
         for r in range(1, S):
             for side in (0, 1):
                 step = 1 if side == 0 else -1
-                ok = s - r >= 0 if side == 0 else s + r < S
 
                 def wait(side=side, step=step, r=r):
                     for j in range(1, G):
@@ -182,185 +192,221 @@
                             groups=g,
                         ).wait_recv()
 
-                when(ok, wait)
+                when(there(side, r), wait)
 
     def begin(array):
         hop(array, 0, 0)
         hop(array, 1, 0)
 
-    begin(0)
-    begin(1)
-
-    def spread(buffer, base):
+    stages = [(0, 1), (2, 3), (4, 5), (6,)]
+    order = [("begin", a, 0) for a in stages[0]]
+    for n, stage in enumerate(stages):
+        for r in range(1, S):
+            order += [("arrive", a, r) for a in stage]
+            if r == max(S - 2, 1) and n + 1 < len(stages):
+                order += [("begin", a, 0) for a in stages[n + 1]]
+    progress = [0]
+
+    def upto(stage, r):
+        goal = max(
+            i for i, (what, a, level) in enumerate(order)
+            if (what == "arrive" and a in stages[stage] and level <= r)
+            or (what == "begin" and stage + 1 < len(stages) and a in stages[stage + 1] and r >= max(S - 2, 1))
+            or (what == "begin" and a in stages[stage])
+        )
+        while progress[0] <= goal:
+            what, a, level = order[progress[0]]
+            if what == "begin":
+                begin(a)
+            else:
+                arrive(a, level)
+            progress[0] += 1
+
+    near, far, end = max(S - 3, 1), max(S - 2, 1), S - 1
+    upto(0, 0)
+
+    def spread(buffer, base, lines):
         def give(source, slot, **where):
             def make():
-                piece = buffer.at[source]
-                return remote(piece, piece, ag_send.at[slot], ag_recv.at[slot], **where)
+                piece = buffer.at[source, lines]
+                return remote(piece, piece, ag_send.at[base, slot], ag_recv.at[base, slot], **where)
 
             send(make)
 
         def take(source, slot):
-            piece = buffer.at[source]
-            remote(piece, piece, ag_send.at[slot], ag_recv.at[slot], tp=t).wait_recv()
+            piece = buffer.at[source, lines]
+            remote(piece, piece, ag_send.at[base, slot], ag_recv.at[base, slot], tp=t).wait_recv()
 
         for i in range(1, T):
-            give(p, base + i, tp=lax.rem(t + i, T))
+            give(p, i, tp=lax.rem(t + i, T))
         for j in range(1, K):
-            give(p, base + T * j, kv=lax.rem(k + j, K))
+            give(p, T * j, kv=lax.rem(k + j, K))
 
         def relay():
             for i in range(1, T):
                 there = lax.rem(t - i + T, T) * K + k
-                take(there, base + i)
+                take(there, i)
                 for j in range(1, K):
-                    give(there, base + T * j + i, kv=lax.rem(k + j, K))
+                    give(there, T * j + i, kv=lax.rem(k + j, K))
 
         def finish():
             for j in range(1, K):
                 for i in range(T):
                     there = lax.rem(t - i + T, T) * K + lax.rem(k - j + K, K)
-                    take(there, base + T * j + i)
+                    take(there, T * j + i)
 
         return relay, finish
 
-    local[0].wait()
-    for j in range(1, S):
+    moves = []
+    for j in range(S):
         came = pl.ds(pl.multiple_of(lax.rem(s - j + S, S) * block, block), block)
-        piece = xb.at[p, came]
-        remote(piece, piece, ev_send.at[j - 1], ev_recv.at[j - 1], seq=s).wait_recv()
-    relay, finish = spread(xb, 0)
+        if j == 0:
+            local[0].wait()
+        else:
+            piece = xb.at[p, came]
+            remote(piece, piece, ev_send.at[j - 1], ev_recv.at[j - 1], seq=s).wait_recv()
+        moves.append(spread(xb, j, came) + (came,))
 
     local[3].wait()
     vocab = table.shape[0]
+    column = jnp.zeros((steps * beams, 1), jnp.int32)
+    line = lax.broadcasted_iota(jnp.int32, column.shape, 0)
+    for r in range(steps * beams):
+        column = jnp.where(line == r, ids[r // beams, r % beams], column)
     onehot = (
-        ids[...] == p * vocab + lax.broadcasted_iota(jnp.int32, (ids.shape[0], vocab), 1)
+        column == p * vocab + lax.broadcasted_iota(jnp.int32, (steps * beams, vocab), 1)
     ).astype(BF16)
     for c in range(TK):
         span = slice(c * cols, (c + 1) * cols)
         look[p, :, span] = dot(onehot, table[:, span]).astype(BF16)
 
-    arrive(0, 1)
-    arrive(1, 1)
-    relay()
+    upto(0, near)
+    for relay, finish, came in moves:
+        relay()
     for slot, other, pt, pk in peers:
 
         def make(slot=slot, pt=pt, pk=pk):
             return remote(look.at[p], look.at[p], lk_send.at[slot], lk_recv.at[slot], tp=pt, kv=pk)
 
         send(make)
-    finish()
-    for c in range(S):
-        lines = slice(c * block, (c + 1) * block)
-        source = [xb[q, lines].astype(F32) for q in range(TK)]
+    upto(0, far)
+    for relay, finish, came in moves:
+        finish()
+        source = [xb[q, came].astype(F32) for q in range(TK)]
         square = sum(jnp.sum(v * v, axis=-1, keepdims=True) for v in source)
         scale = lax.rsqrt(square / width + eps)
         for q in range(TK):
             span = slice(q * cols, (q + 1) * cols)
-            normed[lines, span] = (source[q] * scale * egain[:, span]).astype(BF16)
-    for r in range(2, S):
-        arrive(0, r)
-        arrive(1, r)
-    begin(2)
-    begin(3)
-    for i in (1, 2, 4):
-        local[i].wait()
+            normed[came, span] = (source[q] * scale * egain[:, span]).astype(BF16)
+    upto(0, end)
+    upto(1, near)
+    local[1].wait()
+    local[4].wait()
     settle(0)
     settle(1)
-
     qs[...] = dot(normed[...], wq[...]).astype(BF16)
-    kn[...] = dot(normed[...], wkv[0]).astype(BF16)
-    vn[...] = dot(normed[...], wkv[1]).astype(BF16)
 
     heads = cols // DH
     ratio = cols // kcols
     limit = counts[0] * BLK
-    chunk = min(128, length)
-    turns = [(a, r) for r in range(1, S) for a in (2, 3)]
-    spots = heads * (length // chunk)
-    done = 0
-    spot = 0
+    chunk = min(share, length)
+    upto(1, far)
+    for h in range(heads):
+        hs = slice(h * DH, (h + 1) * DH)
+        ks = slice(h // ratio * DH, (h // ratio + 1) * DH)
+        for c in range(length // chunk):
+            lines = slice(c * chunk, (c + 1) * chunk)
+            old[h, lines] = jnp.exp(dot_t(qs[lines, hs], hist[0, :, ks]) * DH ** (-0.5))
+    upto(1, end)
+    local[2].wait()
+    settle(2)
+    kn[...] = dot(normed[...], wkv[0]).astype(BF16)
+    upto(2, near)
+    settle(3)
+    vn[...] = dot(normed[...], wkv[1]).astype(BF16)
+
+    marks = {1: (2, far), max(heads // 2, 1): (2, end)}
     for h in range(heads):
         hs = slice(h * DH, (h + 1) * DH)
         ks = slice(h // ratio * DH, (h // ratio + 1) * DH)
         for c in range(length // chunk):
             lines = slice(c * chunk, (c + 1) * chunk)
             reach = (c + 1) * chunk
-            q = qs[lines, hs]
-            old = jnp.exp(dot_t(q, hist[0, :, ks]) * DH ** (-0.5))
-            new = jnp.exp(dot_t(q, kn[:reach, ks]) * DH ** (-0.5))
+            new = jnp.exp(dot_t(qs[lines, hs], kn[:reach, ks]) * DH ** (-0.5))
             qi = lax.broadcasted_iota(jnp.int32, (chunk, reach), 0) + c * chunk
             ki = lax.broadcasted_iota(jnp.int32, (chunk, reach), 1)
             new = jnp.where((ki <= qi) & (ki < limit), new, 0.0)
-            total = jnp.sum(old, axis=-1, keepdims=True) + jnp.sum(new, axis=-1, keepdims=True)
+            past = old[h, lines]
+            total = jnp.sum(past, axis=-1, keepdims=True) + jnp.sum(new, axis=-1, keepdims=True)
             att[lines, hs] = (
-                dot((old / total).astype(BF16), hist[1, :, ks])
+                dot((past / total).astype(BF16), hist[1, :, ks])
                 + dot((new / total).astype(BF16), vn[:reach, ks])
             ).astype(BF16)
-            spot += 1
-            while done * spots < (spot - spots // 4) * len(turns):
-                arrive(*turns[done])
-                done += 1
-    while done < len(turns):
-        arrive(*turns[done])
-        done += 1
+        if h + 1 < heads and h + 1 in marks:
+            upto(*marks[h + 1])
+    upto(2, end)
+    upto(3, near)
     local[5].wait()
-    settle(2)
-
-    def project(which):
-        lines = pl.ds(pl.multiple_of(which * share, share), share)
-        for c in range(TK):
-            span = slice(c * cols, (c + 1) * cols)
-            gterm[which, :, span] = dot_t(att[lines, :], wo[span, :]).astype(BF16)
-
-    for j in range(1, K):
-        pk = lax.rem(k + j, K)
+    settle(4)
+    settle(5)
+
+    def lines_of(which):
+        return pl.ds(pl.multiple_of(which * share, share), share)
+
+    def pass_on(c):
+        span = slice(c * cols, (c + 1) * cols)
         for i in range(T):
             it = lax.rem(t + 1 + i, T)
-            project(it * K + pk)
-
-            def make(j=j, i=i, pk=pk, it=it):
-                return remote(
-                    gterm.at[it * K + pk], rk.at[j - 1, i], rk_send.at[j - 1, i], rk_recv.at[j - 1, i], kv=pk
-                )
-
-            send(make)
-    for i in range(T):
-        project(lax.rem(t + 1 + i, T) * K + k)
-    total = None
-    for i in range(T):
+            for j in range(1, K):
+                piece = rk.at[c, j - 1, i]
+                remote(piece, piece, rk_send.at[c, j - 1, i], rk_recv.at[c, j - 1, i], kv=k).wait_recv()
+            total = gterm[c, lines_of(it * K + k)].astype(F32)
+            for j in range(1, K):
+                total = total + rk[c, j - 1, i].astype(F32)
+            if i < T - 1:
+                s1[c, i] = total.astype(BF16)
+
+                def make(i=i, it=it):
+                    return remote(s1.at[c, i], rt.at[c, i], rt_send.at[c, i], rt_recv.at[c, i], tp=it)
+
+                send(make)
+            else:
+                mixed_ref[:, span] = total
+
+    for c in range(TK):
+        gterm[c] = dot_t(att[...], wo[c * cols : (c + 1) * cols, :]).astype(BF16)
         for j in range(1, K):
-            piece = rk.at[j - 1, i]
-            remote(piece, piece, rk_send.at[j - 1, i], rk_recv.at[j - 1, i], kv=k).wait_recv()
-        it = lax.rem(t + 1 + i, T)
-        total = gterm[it * K + k].astype(F32)
-        for j in range(1, K):
-            total = total + rk[j - 1, i].astype(F32)
-        if i < T - 1:
-            s1[i] = total.astype(BF16)
-
-            def make(i=i, it=it):
-                return remote(s1.at[i], rt.at[i], rt_send.at[i], rt_recv.at[i], tp=it)
-
-            send(make)
-        else:
-            mixed_ref[...] = total
-    for i in range(T - 1):
-        remote(rt.at[i], rt.at[i], rt_send.at[i], rt_recv.at[i], tp=t).wait_recv()
-    total = mixed_ref[...]
-    for i in range(T - 1):
-        total = total + rt[i].astype(F32)
-    mine = pl.ds(pl.multiple_of(p * share, share), share)
-    mixed_ref[...] = total
+            pk = lax.rem(k + j, K)
+            for i in range(T):
+
+                def make(c=c, j=j, i=i, pk=pk):
+                    return remote(
+                        gterm.at[c, lines_of(lax.rem(t + 1 + i, T) * K + pk)], rk.at[c, j - 1, i],
+                        rk_send.at[c, j - 1, i], rk_recv.at[c, j - 1, i], kv=pk,
+                    )
+
+                send(make)
+        if c > 0:
+            pass_on(c - 1)
+    pass_on(TK - 1)
+    upto(3, far)
     square = jnp.zeros((share, 1), F32)
+    mine = lines_of(p)
     for q in range(TK):
+        for i in range(T - 1):
+            remote(rt.at[q, i], rt.at[q, i], rt_send.at[q, i], rt_recv.at[q, i], tp=t).wait_recv()
         span = slice(q * cols, (q + 1) * cols)
-        value = mixed_ref[:, span] + xb[q, mine].astype(F32)
+        value = mixed_ref[:, span]
+        for i in range(T - 1):
+            value = value + rt[q, i].astype(F32)
+        value = value + xb[q, mine].astype(F32)
         mixed_ref[:, span] = value
         square = square + jnp.sum(value * value, axis=-1, keepdims=True)
         enc_out[:, span] = value.astype(BF16)
     scale = lax.rsqrt(square / width + eps)
     cx[p] = (mixed_ref[...] * scale * cgain[...]).astype(BF16)
-    relay, finish = spread(cx, TK)
+    relay, finish = spread(cx, S, pl.ds(0, share))
+    upto(3, end)
 
     local[7].wait()
     local[8].wait()
@@ -380,12 +426,11 @@
     queries = query()
     relay()
     local[6].wait()
-    settle(3)
+    settle(6)
     finish()
-    for q in range(TK):
-        lines = slice(q * share, (q + 1) * share)
-        ck[lines] = dot(cx[q], wc[0]).astype(BF16)
-        cv[lines] = dot(cx[q], wc[1]).astype(BF16)
+    across_in = cx[...].reshape(length, width)
+    ck[...] = dot(across_in, wc[0]).astype(BF16)
+    cv[...] = dot(across_in, wc[1]).astype(BF16)
 
     live = lax.broadcasted_iota(jnp.int32, (ratio * beams, length), 1) < limit
     for level in range(steps):
@@ -413,9 +458,12 @@
                     )
 
                 send(make)
-            lines = slice(level * beams, (level + 1) * beams)
+            column = jnp.zeros((beams, 1), jnp.int32)
+            line = lax.broadcasted_iota(jnp.int32, column.shape, 0)
+            for r in range(beams):
+                column = jnp.where(line == r, parents[level, r], column)
             pick = (
-                parents[lines, :] == lax.broadcasted_iota(jnp.int32, (beams, beams), 1)
+                column == lax.broadcasted_iota(jnp.int32, (beams, beams), 1)
             ).astype(F32)
             nextcode = code(level + 1)
             for slot, other, pt, pk in peers:
@@ -481,27 +529,29 @@
                 jax.ShapeDtypeStruct((share, width), BF16),
                 jax.ShapeDtypeStruct((beams, cols), BF16),
             ),
-            in_specs=[anywhere, anywhere, smem, vmem, vmem] + [anywhere] * 7 + [vmem] * 3,
+            in_specs=[anywhere, anywhere, smem, smem, smem] + [anywhere] * 7 + [vmem] * 3,
             out_specs=(vmem, vmem),
             scratch_shapes=[
                 vm(width, cols), vm(2, width, kcols), vm(width, cols), vm(2, width, kcols),
                 vm(width, cols), vm(width, cols), vm(*table.shape), vm(2, hist_len, kcols),
                 vm(TK, length, cols), vm(length, width),
                 vm(length, cols), vm(length, kcols), vm(length, kcols), vm(length, cols),
-                vm(TK, share, width), vm(max(K - 1, 1), T, share, width), vm(max(T - 1, 1), share, width),
-                vm(max(T - 1, 1), share, width), vm(TK, share, width), vm(length, kcols), vm(length, kcols),
+                vm(TK, length, cols), vm(TK, max(K - 1, 1), T, share, cols), vm(TK, max(T - 1, 1), share, cols),
+                vm(TK, max(T - 1, 1), share, cols), vm(TK, share, width), vm(length, kcols), vm(length, kcols),
                 vm(TK, steps * beams, width), vm(steps, TK, beams, width),
                 vm(TK, beams, cols), vm(TK, beams, cols),
                 vf(beams, width), vf(share, width), vm(beams, cols),
-                dma(9), dma(4, 2, S), dma(4, 2, S), dma(4, 2, S, G), dma(4, 2, S, G), dma(S), dma(S),
-                dma(2 * TK), dma(2 * TK), dma(TK), dma(TK), dma(K, T), dma(K, T), dma(T), dma(T),
+                vf(cols // DH, length, hist_len),
+                dma(9), dma(7, 2, S), dma(7, 2, S), dma(7, 2, S, G), dma(7, 2, S, G), dma(S), dma(S),
+                dma(S + 1, TK), dma(S + 1, TK), dma(TK), dma(TK), dma(TK, K, T), dma(TK, K, T), dma(TK, T),
+                dma(TK, T),
                 dma(steps, TK), dma(steps, TK),
             ],
             compiler_params=pltpu.CompilerParams(
                 collective_id=0, has_side_effects=True, vmem_limit_bytes=60 * 1024 * 1024
             ),
         )(
-            events, history, counts, ids.reshape(-1, 1), parents.reshape(-1, 1), wq, wkv, wo, wc, dq, do,
+            events, history, counts, ids, parents, wq, wkv, wo, wc, dq, do,
             table, egain[None], cgain[None], dgain[None],
         )
         return enc[None], beam

time: 154 us -> 140 us (0.909)
  Pallas kernels: 147 us -> 135 us
  local copies, waits for them, and re-layouts: 5.97 us -> 3.2 us
    pallas_call x1, Pallas kernels: 147 us -> 135 us  [shards(): pl.pallas_call(functools.partial(body, (G, S, T, K)), out_shape=(jax.Shap...]
    reshape x2 -> x0, local copies, waits for them, and re-layouts: 2.77 us -> none  [the longest x1 1.38 us: shards(): ids.reshape(-1, 1)]
where the time goes in v2:
time: 140 us; the launch traced here: 139 us
  Pallas kernels  135 us (96%)
  local copies, waits for them, and re-layouts  3.2 us (2%)
    pallas_call x1, Pallas kernels, shards(): pl.pallas_call(functools.partial(body, (G, S, T, K)), out_shape=(jax.Shap...  135 us
    unnamed x2, local copies, waits for them, and re-layouts  3.2 us

profile of v2, /device:TPU:0, one launch (start us, length us, event | category | flops | bytes accessed | tf_op | source)
XLA Modules:
  0.0 139.2 jit_solution(8172007126899402541)
XLA Ops:
  1.3 134.7 %shard_map.158 = (bf16[128,2048]{1,0:T(8,128)(2,1)}, bf16[16,512]{1,0:T(8,128)(2,1)}) custom-call(bf16[4,128,512]{2,1,0:T(8,128)(2,1)} %events.1, bf16[2,1,512,256]{3,2,1,0:T(8,128)(2,1)} %history.1, s32[1]{0:T(128)S(6)} %copy.19.counts, s32[4,16]{1,0:T(4,128)} %ids.1, s32[3,16]{1,0:T(4,128)} %parents.1, bf16[512,512]{1,0:T(8,128)(2,1)} %wq_in.1, ...), custom_call_target="tpu_custom_call" | custom-call | tf_op jit(solution)/shard_map/pallas_call | solution.py:526
  136.0 1.9 %copy.20 = bf16[1,128,2048]{2,1,0:T(8,128)(2,1)} copy(bf16[1,128,2048]{2,1,0:T(8,128)(2,1)} %bitcast.4) | data formatting | bytes 1048576
  137.9 1.3 copy.21

commit v3 on v2

--- a/solution.py
+++ b/solution.py
@@ -203,7 +203,7 @@
     for n, stage in enumerate(stages):
         for r in range(1, S):
             order += [("arrive", a, r) for a in stage]
-            if r == max(S - 2, 1) and n + 1 < len(stages):
+            if r == max(S - 2, 1) and 0 < n < len(stages) - 1:
                 order += [("begin", a, 0) for a in stages[n + 1]]
     progress = [0]
 
@@ -224,6 +224,8 @@
 
     near, far, end = max(S - 3, 1), max(S - 2, 1), S - 1
     upto(0, 0)
+    for a in stages[1]:
+        begin(a)
 
     def spread(buffer, base, lines):
         def give(source, slot, **where):
@@ -267,6 +269,7 @@
             remote(piece, piece, ev_send.at[j - 1], ev_recv.at[j - 1], seq=s).wait_recv()
         moves.append(spread(xb, j, came) + (came,))
 
+    upto(0, near)
     local[3].wait()
     vocab = table.shape[0]
     column = jnp.zeros((steps * beams, 1), jnp.int32)
@@ -280,7 +283,6 @@
         span = slice(c * cols, (c + 1) * cols)
         look[p, :, span] = dot(onehot, table[:, span]).astype(BF16)
 
-    upto(0, near)
     for relay, finish, came in moves:
         relay()
     for slot, other, pt, pk in peers:

time: 140 us -> 143 us (1.021)
  Pallas kernels: 135 us -> 139 us
    pallas_call x1, Pallas kernels: 135 us -> 139 us  [shards(): pl.pallas_call(functools.partial(body, (G, S, T, K)), out_shape=(jax.Shap...]
where the time goes in v3:
time: 143 us
  Pallas kernels  139 us (97%)
  local copies, waits for them, and re-layouts  3.2 us (2%)
    pallas_call x1, Pallas kernels, shards(): pl.pallas_call(functools.partial(body, (G, S, T, K)), out_shape=(jax.Shap...  139 us
    unnamed x2, local copies, waits for them, and re-layouts  3.2 us

profile of v3, /device:TPU:0, one launch (start us, length us, event | category | flops | bytes accessed | tf_op | source)
XLA Modules:
  0.0 143.0 jit_solution(13225584365684186246)
XLA Ops:
  1.3 138.5 %shard_map.158 = (bf16[128,2048]{1,0:T(8,128)(2,1)}, bf16[16,512]{1,0:T(8,128)(2,1)}) custom-call(bf16[4,128,512]{2,1,0:T(8,128)(2,1)} %events.1, bf16[2,1,512,256]{3,2,1,0:T(8,128)(2,1)} %history.1, s32[1]{0:T(128)S(6)} %copy.19.counts, s32[4,16]{1,0:T(4,128)} %ids.1, s32[3,16]{1,0:T(4,128)} %parents.1, bf16[512,512]{1,0:T(8,128)(2,1)} %wq_in.1, ...), custom_call_target="tpu_custom_call" | custom-call | tf_op jit(solution)/shard_map/pallas_call | solution.py:528
  139.8 1.9 %copy.20 = bf16[1,128,2048]{2,1,0:T(8,128)(2,1)} copy(bf16[1,128,2048]{2,1,0:T(8,128)(2,1)} %bitcast.4) | data formatting | bytes 1048576
  141.7 1.3 copy.21
